TPU v7x, 32 devices: a whole 2x2x4 slice. The times are simulated.
32 devices in a mesh: dp: 2 (over x), mp: 16 (over z, y, core).
Axes of the slice: x: 2, y: 2, z: 4, core: 2. Of those that a mesh axis runs over, the one named last changes fastest.
Arguments:
- tokens: bfloat16 [32, 512, 768], P(('dp', 'mp')), may hold values from -6 to 6
- segment_ids: int32 [32, 512], P(('dp', 'mp')), may hold values from 0 to 3, never falling along the last dimension, each value on 1 to 256 neighbouring positions
- swap_step: int32 [1], replicated, may hold values from 0 to 1023
- feature_bank: bfloat16 [8, 12, 64, 64], replicated, may hold values from -5 to 5
- query_weight: bfloat16 [768, 768], replicated, may hold values from -0.21875 to 0.21875
- query_bias: bfloat16 [768], replicated, may hold values from -1.5 to 1.5
- key_weight: bfloat16 [768, 768], replicated, may hold values from -0.21875 to 0.21875
- value_weight: bfloat16 [768, 768], replicated, may hold values from -0.21875 to 0.21875
- value_bias: bfloat16 [768], replicated, may hold values from -1.5 to 1.5
- out_weight: bfloat16 [768, 768], replicated, may hold values from -0.875 to 0.875
- out_bias: bfloat16 [768], replicated, may hold values from -1.5 to 1.5
- position_logits: bfloat16 [12, 1023], replicated, may hold values from -3 to 3
- first_gain: bfloat16 [768], replicated, may hold values from 0.5 to 1.5
- first_shift: bfloat16 [768], replicated, may hold values from -1.5 to 1.5
- up_weight: bfloat16 [768, 3072], P(None, 'mp'), may hold values from -0.21875 to 0.21875
- up_bias: bfloat16 [3072], P('mp'), may hold values from -1.5 to 1.5
- down_weight: bfloat16 [3072, 768], P('mp'), may hold values from -0.109375 to 0.109375
- down_bias: bfloat16 [768], replicated, may hold values from -1.5 to 1.5
- second_gain: bfloat16 [768], replicated, may hold values from 0.5 to 1.5
- second_shift: bfloat16 [768], replicated, may hold values from -1.5 to 1.5
- out_cotangent: bfloat16 [32, 512, 768], P(('dp', 'mp')), may hold values from -6 to 6
Outputs:
- layer_out: bfloat16 [32, 512, 768], P(('dp', 'mp'))
- grad_tokens: float32 [32, 512, 768], P(('dp', 'mp'))
- grad_query_weight: float32 [768, 768], replicated
- grad_query_bias: float32 [768], replicated
- grad_key_weight: float32 [768, 768], replicated
- grad_value_weight: float32 [768, 768], replicated
- grad_value_bias: float32 [768], replicated
- grad_out_weight: float32 [768, 768], replicated
- grad_out_bias: float32 [768], replicated
- grad_position_logits: float32 [12, 1023], replicated
- grad_first_gain: float32 [768], replicated
- grad_first_shift: float32 [768], replicated
- grad_up_weight: float32 [768, 3072], P(None, 'mp')
- grad_up_bias: float32 [3072], P('mp')
- grad_down_weight: float32 [3072, 768], P('mp')
- grad_down_bias: float32 [768], replicated
- grad_second_gain: float32 [768], replicated
- grad_second_shift: float32 [768], replicated
Inputs may be any that keep to these rules, and one draw needn't show every extreme that they name: `segment_ids`: within each row the ids never fall; a document holds at most 256 tokens.
All inputs are finite; a program needn't handle non-finite values.
Results may differ from a plain program's by a relative error of at most 0.02.
Values may be sent and summed in bfloat16 or wider, within the bound.
No kernel may reach another device: no remote copies, remote signals or barrier semaphores. Data moves between devices by JAX's collectives and lax.ppermute only.
A program may use at most 320 MiB of HBM per device.

v0:
```python
import jax
import jax.numpy as jnp
from jax import lax
from jax.sharding import PartitionSpec as P

EPSILON = 1e-05


def dot_first(left_side, right_side):
    return lax.dot_general(
        left_side, right_side, (((0,), (0,)), ((), ())), preferred_element_type=jnp.float32
    )


def dot_last(left_side, right_side):
    return lax.dot_general(
        left_side, right_side, (((1,), (1,)), ((), ())), preferred_element_type=jnp.float32
    )


def toeplitz(entries):
    head_count, span = entries.shape
    length = (span + 1) // 2
    rolled = jnp.roll(entries[:, ::-1], length, axis=1)
    tiled = jnp.tile(rolled, (1, length))[:, : length * (span - 1)]
    return tiled.reshape(head_count, length, span - 1)[:, :, :length]


def normalize(inputs, factor, offset):
    centre = inputs - jnp.mean(inputs, axis=-1, keepdims=True)
    spread = jnp.mean(centre * centre, axis=-1, keepdims=True)
    inverse = lax.rsqrt(spread + EPSILON)
    normed = centre * inverse
    return (normed * factor + offset, normed, inverse)


def norm_back(upstream, normed, inverse, factor):
    scaled = upstream * factor
    inner = (
        scaled
        - jnp.mean(scaled, axis=-1, keepdims=True)
        - normed * jnp.mean(scaled * normed, axis=-1, keepdims=True)
    )
    return (inverse * inner, jnp.sum(upstream * normed, axis=0), jnp.sum(upstream, axis=0))


def lift(row_block, projection):
    lifted = jnp.einsum("lhd,hdm->hlm", row_block, projection, preferred_element_type=jnp.float32)
    widened = row_block.astype(jnp.float32)
    squares = jnp.einsum("lhd,lhd->hl", widened, widened)
    return jnp.exp(lifted - 0.5 * squares[:, :, None]) * projection.shape[-1] ** (-0.5)


def lift_back(row_block, projection, feature, grad_feature):
    product = grad_feature.astype(jnp.float32) * feature
    rounded = product.astype(jnp.bfloat16)
    through = jnp.einsum("hlm,hdm->lhd", rounded, projection, preferred_element_type=jnp.float32)
    return through - row_block.astype(jnp.float32) * jnp.sum(product, axis=-1).T[:, :, None]


def row_scores(row_queries, row_keys, row_values, row_segments, projection, position_table):
    query_feat = lift(row_queries, projection)
    key_feat = lift(row_keys, projection)
    query_low = query_feat.astype(jnp.bfloat16)
    key_low = key_feat.astype(jnp.bfloat16)
    same_doc = (row_segments[:, None] == row_segments[None, :]).astype(jnp.float32)
    kernel = jnp.einsum("hlm,hkm->hlk", query_low, key_low, preferred_element_type=jnp.float32)
    weights = kernel * position_table * same_doc[None]
    denominator = jnp.sum(weights, axis=-1)
    weights_low = weights.astype(jnp.bfloat16)
    numerator = jnp.einsum(
        "hlk,khd->lhd", weights_low, row_values, preferred_element_type=jnp.float32
    )
    return (
        query_feat,
        key_feat,
        query_low,
        key_low,
        same_doc,
        kernel,
        weights_low,
        denominator,
        numerator,
    )


def local(
    tokens,
    segment_ids,
    swap_step,
    feature_bank,
    query_weight,
    query_bias,
    key_weight,
    value_weight,
    value_bias,
    out_weight,
    out_bias,
    position_logits,
    first_gain,
    first_shift,
    up_weight,
    up_bias,
    down_weight,
    down_bias,
    second_gain,
    second_shift,
    out_cotangent,
):
    rows_here, length, model_width = tokens.shape
    head_count = position_logits.shape[0]
    head_size = model_width // head_count
    query_scale = head_size ** (-0.25)
    token_rows = tokens.reshape(-1, model_width)
    projection = lax.dynamic_index_in_dim(
        feature_bank, swap_step[0] % feature_bank.shape[0], 0, keepdims=False
    )
    entries = jnp.exp(position_logits.astype(jnp.float32))
    position_table = toeplitz(entries)

    def by_heads(array):
        return array.reshape(rows_here, length, head_count, head_size)

    queries = (
        (
            jnp.dot(token_rows, query_weight, preferred_element_type=jnp.float32)
            + query_bias.astype(jnp.float32)
        )
        * query_scale
    ).astype(jnp.bfloat16)
    keys_all = (
        jnp.dot(token_rows, key_weight, preferred_element_type=jnp.float32) * query_scale
    ).astype(jnp.bfloat16)
    values = (
        jnp.dot(token_rows, value_weight, preferred_element_type=jnp.float32)
        + value_bias.astype(jnp.float32)
    ).astype(jnp.bfloat16)

    def forward_row(pieces):
        row_queries, row_keys, row_values, row_segments = pieces
        scores = row_scores(
            row_queries, row_keys, row_values, row_segments, projection, position_table
        )
        return (scores[8] / scores[7].T[:, :, None]).astype(jnp.bfloat16)

    mixed_out = lax.map(
        forward_row, (by_heads(queries), by_heads(keys_all), by_heads(values), segment_ids)
    ).reshape(-1, model_width)
    branch = jnp.dot(mixed_out, out_weight, preferred_element_type=jnp.float32) + out_bias.astype(
        jnp.float32
    )
    first_factor = first_gain.astype(jnp.float32)
    hidden, first_normed, first_inverse = normalize(
        token_rows.astype(jnp.float32) + branch, first_factor, first_shift.astype(jnp.float32)
    )
    hidden_low = hidden.astype(jnp.bfloat16)
    gathered = lax.all_gather(hidden_low, "mp", axis=0, tiled=True)
    upward = jnp.dot(gathered, up_weight, preferred_element_type=jnp.float32) + up_bias.astype(
        jnp.float32
    )
    activated = jax.nn.gelu(upward, approximate=False).astype(jnp.bfloat16)
    feed_out = lax.psum_scatter(
        jnp.dot(activated, down_weight, preferred_element_type=jnp.float32),
        "mp",
        scatter_dimension=0,
        tiled=True,
    )
    second_factor = second_gain.astype(jnp.float32)
    summed = hidden + feed_out + down_bias.astype(jnp.float32)
    layer_out, second_normed, second_inverse = normalize(
        summed, second_factor, second_shift.astype(jnp.float32)
    )
    upstream = out_cotangent.reshape(-1, model_width).astype(jnp.float32)
    grad_summed, grad_second_gain, grad_second_shift = norm_back(
        upstream, second_normed, second_inverse, second_factor
    )
    grad_down_bias = jnp.sum(grad_summed, axis=0)
    grad_feed = grad_summed.astype(jnp.bfloat16)

    def gelu_exact(inputs):
        return jax.nn.gelu(inputs, approximate=False)

    grad_gathered = lax.all_gather(grad_feed, "mp", axis=0, tiled=True)
    grad_act = dot_last(grad_gathered, down_weight)
    grad_upward = jax.vjp(gelu_exact, upward)[1](grad_act)[0].astype(jnp.bfloat16)
    part_up_weight = dot_first(gathered, grad_upward)
    part_down_weight = dot_first(activated, grad_gathered)
    part_up_bias = jnp.sum(grad_upward.astype(jnp.float32), axis=0)
    grad_hidden_ffn = lax.psum_scatter(
        dot_last(grad_upward, up_weight), "mp", scatter_dimension=0, tiled=True
    )
    grad_up_weight, grad_up_bias, grad_down_weight = lax.psum(
        (part_up_weight, part_up_bias, part_down_weight), "dp"
    )
    grad_hidden = grad_summed + grad_hidden_ffn
    grad_residual, grad_first_gain, grad_first_shift = norm_back(
        grad_hidden, first_normed, first_inverse, first_factor
    )
    grad_branch = grad_residual.astype(jnp.bfloat16)
    grad_out_bias = jnp.sum(grad_branch.astype(jnp.float32), axis=0)
    grad_out_weight = dot_first(mixed_out, grad_branch)
    grad_mixed = dot_last(grad_branch, out_weight).astype(jnp.bfloat16)

    def backward_row(running, pieces):
        row_queries, row_keys, row_values, row_segments, row_grad = pieces
        (
            query_feat,
            key_feat,
            query_low,
            key_low,
            same_doc,
            kernel,
            weights_low,
            denominator,
            numerator,
        ) = row_scores(row_queries, row_keys, row_values, row_segments, projection, position_table)
        spread_denom = denominator.T[:, :, None]
        grad_wide = row_grad.astype(jnp.float32)
        grad_numer = (grad_wide / spread_denom).astype(jnp.bfloat16)
        grad_denom = -jnp.einsum("lhd,lhd->hl", grad_wide, numerator / spread_denom) / denominator
        grad_weights = (
            jnp.einsum("lhd,khd->hlk", grad_numer, row_values, preferred_element_type=jnp.float32)
            + grad_denom[:, :, None]
        )
        grad_values = jnp.einsum(
            "hlk,lhd->khd", weights_low, grad_numer, preferred_element_type=jnp.float32
        ).astype(jnp.bfloat16)
        masked = grad_weights * same_doc[None]
        grad_kernel = (masked * position_table).astype(jnp.bfloat16)
        running = running + masked * kernel
        grad_qfeat = jnp.einsum(
            "hlk,hkm->hlm", grad_kernel, key_low, preferred_element_type=jnp.float32
        ).astype(jnp.bfloat16)
        grad_kfeat = jnp.einsum(
            "hlk,hlm->hkm", grad_kernel, query_low, preferred_element_type=jnp.float32
        ).astype(jnp.bfloat16)
        grad_queries = lift_back(row_queries, projection, query_feat, grad_qfeat).astype(
            jnp.bfloat16
        )
        grad_keys = lift_back(row_keys, projection, key_feat, grad_kfeat).astype(jnp.bfloat16)
        return (running, (grad_queries, grad_keys, grad_values))

    start_table = jnp.zeros((head_count, length, length), jnp.float32)
    table_grad, row_grads = lax.scan(
        backward_row,
        start_table,
        (
            by_heads(queries),
            by_heads(keys_all),
            by_heads(values),
            segment_ids,
            by_heads(grad_mixed),
        ),
    )
    grad_queries = row_grads[0].reshape(-1, model_width)
    grad_keys = row_grads[1].reshape(-1, model_width)
    grad_values = row_grads[2].reshape(-1, model_width)
    grad_query_weight = dot_first(token_rows, grad_queries) * query_scale
    grad_query_bias = jnp.sum(grad_queries.astype(jnp.float32), axis=0) * query_scale
    grad_key_weight = dot_first(token_rows, grad_keys) * query_scale
    grad_value_weight = dot_first(token_rows, grad_values)
    grad_value_bias = jnp.sum(grad_values.astype(jnp.float32), axis=0)
    grad_tokens = (
        grad_residual
        + query_scale * (dot_last(grad_queries, query_weight) + dot_last(grad_keys, key_weight))
        + dot_last(grad_values, value_weight)
    )
    toeplitz_back = jax.vjp(toeplitz, entries)[1]
    grad_logits = toeplitz_back(table_grad)[0] * entries
    shared = lax.psum(
        (
            grad_query_weight,
            grad_query_bias,
            grad_key_weight,
            grad_value_weight,
            grad_value_bias,
            grad_out_weight,
            grad_out_bias,
            grad_logits,
            grad_first_gain,
            grad_first_shift,
            grad_down_bias,
            grad_second_gain,
            grad_second_shift,
        ),
        ("dp", "mp"),
    )
    return (
        layer_out.astype(jnp.bfloat16).reshape(rows_here, length, model_width),
        grad_tokens.reshape(rows_here, length, model_width),
        shared[0],
        shared[1],
        shared[2],
        shared[3],
        shared[4],
        shared[5],
        shared[6],
        shared[7],
        shared[8],
        shared[9],
        grad_up_weight,
        grad_up_bias,
        grad_down_weight,
        shared[10],
        shared[11],
        shared[12],
    )


def solution(mesh):
    in_specs = (
        P(("dp", "mp"), None, None),
        P(("dp", "mp"), None),
        P(),
        P(),
        P(),
        P(),
        P(),
        P(),
        P(),
        P(),
        P(),
        P(),
        P(),
        P(),
        P(None, "mp"),
        P("mp"),
        P("mp", None),
        P(),
        P(),
        P(),
        P(("dp", "mp"), None, None),
    )
    out_specs = (
        P(("dp", "mp"), None, None),
        P(("dp", "mp"), None, None),
        P(),
        P(),
        P(),
        P(),
        P(),
        P(),
        P(),
        P(),
        P(),
        P(),
        P(None, "mp"),
        P("mp"),
        P("mp", None),
        P(),
        P(),
        P(),
    )
    return jax.shard_map(local, mesh=mesh, in_specs=in_specs, out_specs=out_specs, check_vma=False)
```

profile of v0, /device:TPU:8, one launch (start us, length us, event | category | flops | bytes accessed | tf_op | source)
XLA Modules:
  0.0 1372.5 jit_solution(12590324390042866375)
XLA Ops:
  20.0 11.5 tile.4
  31.5 38.0 %tile.10 = f32[12,523776]{1,0:T(8,128)} reshape(f32[12,512,1023]{2,1,0:T(8,128)} %tile.4) | data formatting | bytes 50282496 | tf_op jit(solution)/shard_map/tile | solution.py:25
  69.5 22.6 %slice.28 = f32[12,523264]{1,0:T(8,128)} slice(f32[12,523776]{1,0:T(8,128)} %tile.10), slice={[0:12], [0:523264]} | slice | bytes 50233344 | tf_op jit(solution)/shard_map/slice | solution.py:25
  92.1 42.2 %reshape.182 = f32[12,512,1022]{2,1,0:T(8,128)} reshape(f32[12,523264]{1,0:T(8,128)} %slice.28) | data formatting | bytes 50233344 | tf_op jit(solution)/shard_map/reshape | solution.py:26
  134.3 10.7 slice.29
  145.0 12.6 copy.112
  166.5 9.4 fusion.7
  182.2 100.6 %all-gather.3.cloned.1.call-done = bf16[8192,768]{1,0:T(8,128)(2,1)} async-done(((bf16[512,768]{1,0:T(8,128)(2,1)}), bf16[8192,768]{1,0:T(8,128)(2,1)}) %all-gather.3.cloned.1.call-update) | async-done | bytes 12582928 | tf_op jit(solution)/shard_map/all_gather | solution.py:157
  282.8 20.5 %multiply_convert_fusion.1 = (bf16[8192,192]{0,1:T(8,128)(2,1)S(1)}, f32[8192,192]{0,1:T(8,128)}, f32[8192,192]{0,1:T(8,128)}) fusion(f32[192]{0:T(256)S(1)} %convert_element_type.196, bf16[8192,768]{1,0:T(8,128)(2,1)} %all-gather.3.cloned.1.call-done, bf16[768,192]{0,1:T(8,128)(2,1)} %param.35), kind=kOutput, calls=%fused_computation.9 | convolution fusion | flops 2519728128 | bytes 28607232 | tf_op jit(solution)/shard_map/dot_general | solution.py:158
  305.1 10.1 fusion.63
  315.9 240.6 %reduce-scatter.3.cloned.1.call-done = f32[512,768]{1,0:T(8,128)} async-done(((f32[8192,768]{1,0:T(8,128)}), f32[512,768]{1,0:T(8,128)}) %reduce-scatter.3.cloned.1.call-update) | async-done | bytes 1572880 | tf_op jit(solution)/shard_map/reduce_scatter | solution.py:162
  565.2 100.3 %all-gather.5.cloned.1.call-done = bf16[8192,768]{1,0:T(8,128)(2,1)} async-done(((bf16[512,768]{1,0:T(8,128)(2,1)}), bf16[8192,768]{1,0:T(8,128)(2,1)}) %all-gather.5.cloned.1.call-update) | async-done | bytes 12582928 | tf_op jit(solution)/shard_map/all_gather | solution.py:183
  665.5 10.9 convert_reduce_fusion
  678.1 10.1 fusion.64
  688.7 240.8 %reduce-scatter.5.cloned.1.call-done = f32[512,768]{1,0:T(8,128)} async-done(((f32[8192,768]{1,0:T(8,128)}), f32[512,768]{1,0:T(8,128)}) %reduce-scatter.5.cloned.1.call-update) | async-done | bytes 1572880 | tf_op jit(solution)/shard_map/reduce_scatter | solution.py:189
  945.8 18.3 %fusion = (f32[12,512,512]{1,2,0:T(8,128)}, bf16[12,512,512]{1,2,0:T(8,128)(2,1)}) fusion(f32[12,512,512]{1,2,0:T(8,128)} %get-tuple-element.152, f32[12,512]{1,0:T(8,128)S(1)} %negate_divide_fusion, f32[512,512]{0,1:T(8,128)} %compare_convert_fusion, f32[12,512,512]{1,2,0:T(8,128)} %copy.112, bf16[512,12,64]{0,2,1:T(8,128)(2,1)} %bitcast.162, ...), kind=kOutput, calls=%fused_computation.3 | convolution fusion | flops 419561472 | bytes 46710784 | tf_op jit(solution)/shard_map/while/body/eval_jaxpr/lhd,khd->hlk/dot_general | solution.py:222
  986.5 9.4 fusion.67
  1004.2 12.8 copy.113
  1017.0 14.6 %pad.14.clone = f32[12,512,1022]{2,1,0:T(8,128)} pad(f32[12,512,512]{2,1,0:T(8,128)} %copy.113, f32[]{:T(128)} %constant.51.clone.1), padding=0_0x0_0x0_510 | pad | bytes 37699588 | tf_op jit(solution)/shard_map/transpose(jvp())/pad | solution.py:26
  1031.6 47.0 %reshape.189 = f32[12,523264]{1,0:T(8,128)} reshape(f32[12,512,1022]{2,1,0:T(8,128)} %pad.14.clone) | data formatting | bytes 50233344 | tf_op jit(solution)/shard_map/transpose(jvp())/reshape | solution.py:26
  1078.6 22.9 %pad.15 = f32[12,523776]{1,0:T(8,128)} pad(f32[12,523264]{1,0:T(8,128)} %reshape.189, f32[]{:T(128)} %constant.51.clone.1), padding=0_0x0_512 | pad | bytes 50257924 | tf_op jit(solution)/shard_map/transpose(jvp())/pad | solution.py:25
  1101.5 43.8 %reshape.190 = f32[12,512,1023]{2,1,0:T(8,128)} reshape(f32[12,523776]{1,0:T(8,128)} %pad.15) | data formatting | bytes 50282496 | tf_op jit(solution)/shard_map/transpose(jvp())/reshape | solution.py:25
  1180.2 36.7 %all-reduce.15.cloned.1.call-done = (f32[768,192]{0,1:T(8,128)}, f32[192,768]{1,0:T(8,128)}) async-done(((f32[768,192]{0,1:T(8,128)}, f32[192,768]{1,0:T(8,128)}), (f32[768,192]{0,1:T(8,128)}, f32[192,768]{1,0:T(8,128)})) %all-reduce.15.cloned.1.call-update) | async-done | bytes 1179664 | tf_op jit(solution)/shard_map/psum | solution.py:192
  1216.9 136.8 %all-reduce.11.cloned.1.call-done = (f32[768]{0:T(1024)}, f32[768]{0:T(1024)}, f32[768]{0:T(1024)}, f32[12,1023]{1,0:T(8,128)}, f32[768]{0:T(1024)}, /*index=5*/...) async-done(((f32[768]{0:T(1024)}, f32[768]{0:T(1024)}, f32[768]{0:T(1024)}, f32[12,1023]{1,0:T(8,128)}, f32[768]{0:T(1024)}, /*index=5*/f32[768]{0:T(1024)}, ...) | async-done | bytes 73696 | tf_op jit(solution)/shard_map/psum | solution.py:270
  (217 shorter events, 133.5 us)
Async XLA Ops:
  7.2 157.0 %copy-start = (bf16[8,12,64,64]{3,2,1,0:T(8,128)(2,1)S(1)}, bf16[8,12,64,64]{3,2,1,0:T(8,128)(2,1)}, u32[]{:S(2)}) copy-start(bf16[8,12,64,64]{3,2,1,0:T(8,128)(2,1)} %param.24) | copy-start | bytes 2359300
  7.2 275.6 %all-gather.3.cloned.1.call-start = ((), (), s32[]{:S(2)}) async-start(), calls=%async_computation.2 | async-start | bytes 13369344 | tf_op jit(solution)/shard_map/all_gather | solution.py:157
  14.2 150.0 %copy-start.9 = (bf16[512,768]{0,1:T(8,128)(2,1)}, bf16[512,768]{0,1:T(8,128)(2,1)S(1)}, u32[]{:S(2)}) copy-start(bf16[512,768]{0,1:T(8,128)(2,1)S(1)} %copy.58) | copy-start | bytes 2359300
  18.8 145.9 %copy-start.11 = (bf16[512,768]{0,1:T(8,128)(2,1)}, bf16[512,768]{0,1:T(8,128)(2,1)S(1)}, u32[]{:S(2)}) copy-start(bf16[512,768]{0,1:T(8,128)(2,1)S(1)} %copy.60) | copy-start | bytes 2359300
  145.0 12.6 copy-start.37
  145.0 13.7 copy-start.44
  164.7 11.2 copy-start.2
  166.5 9.4 copy-start.4
  166.5 9.4 copy-start.26
  182.1 374.4 %reduce-scatter.3.cloned.1.call-start = ((), (), s32[]{:S(2)}) async-start(), calls=%async_computation.3 | async-start | bytes 26738688 | tf_op jit(solution)/shard_map/reduce_scatter | solution.py:162
  182.1 123.0 %copy-start.32 = (bf16[192,768]{1,0:T(8,128)(2,1)S(1)}, bf16[192,768]{1,0:T(8,128)(2,1)}, u32[]{:S(2)}) copy-start(bf16[192,768]{1,0:T(8,128)(2,1)} %param.37) | copy-start | bytes 884740
  315.2 350.3 %all-gather.5.cloned.1.call-start = ((), (), s32[]{:S(2)}) async-start(), calls=%async_computation.4 | async-start | bytes 13369344 | tf_op jit(solution)/shard_map/all_gather | solution.py:183
  565.2 364.3 %reduce-scatter.5.cloned.1.call-start = ((), (), s32[]{:S(2)}) async-start(), calls=%async_computation.5 | async-start | bytes 26738688 | tf_op jit(solution)/shard_map/reduce_scatter | solution.py:189
  665.5 12.5 copy-start.33
  688.2 482.9 %all-reduce.13.cloned.1.call-start = ((), (), s32[]{:S(2)}) async-start(), calls=%async_computation.7 | async-start | bytes 18874368 | tf_op jit(solution)/shard_map/psum | solution.py:270
  938.1 7.7 copy-start.16
  945.8 18.3 %copy-start.3 = (f32[12,512,64]{1,2,0:T(8,128)S(1)}, f32[12,512,64]{1,2,0:T(8,128)}, u32[]{:S(2)}) copy-start(f32[12,512,64]{1,2,0:T(8,128)} %copy-done.2) | copy-start | bytes 4718596
  945.8 18.3 %copy-start.5 = (f32[12,512,64]{1,2,0:T(8,128)S(1)}, f32[12,512,64]{1,2,0:T(8,128)}, u32[]{:S(2)}) copy-start(f32[12,512,64]{1,2,0:T(8,128)} %copy-done.4) | copy-start | bytes 4718596
  979.1 237.9 %all-reduce.15.cloned.1.call-start = ((), (), s32[]{:S(2)}) async-start(), calls=%async_computation.8 | async-start | bytes 2359296 | tf_op jit(solution)/shard_map/psum | solution.py:192
  986.5 9.4 copy-start.23
  1004.1 349.6 %all-reduce.11.cloned.1.call-start = ((), (), s32[]{:S(2)}) async-start(), calls=%async_computation.6 | async-start | bytes 196608 | tf_op jit(solution)/shard_map/psum | solution.py:270
  1145.4 11.2 copy-start.35
  1356.3 5.7 copy-start.31
  1359.6 5.3 copy-start.38
  (40 other events, 91.7 us)
Sparse Core Ops, SparseCore 0:
  182.2 100.5 all-gather.2
  315.3 241.1 reduce-scatter.2
  565.3 100.1 all-gather.4
  688.3 241.0 reduce-scatter.4
  979.2 191.8 all-reduce.12
  1173.9 42.9 all-reduce.14
  1225.0 128.6 all-reduce.10
where the time goes:
time: 1380 us; the launch traced here: 1370 us
  waiting for transfers between devices  860 us (62%)
  local copies, waits for them, and re-layouts  320 us (23%)
  matrix products  142 us (10%)
  other arithmetic  28.3 us (2%)
  between operations  15.7 us (1%)
    reduce_scatter x1, waiting for transfers between devices, local(): lax.psum_scatter(dot_last(grad_upward, up_weight), 'mp', scatter_dimensio...  241 us
    reduce_scatter x1, waiting for transfers between devices, local(): lax.psum_scatter(jnp.dot(activated, down_weight, preferred_element_type=j...  241 us
    psum x2, waiting for transfers between devices, local(): lax.psum((grad_query_weight, grad_query_bias, grad_key_weight, grad_value...  141 us
    all_gather x1, waiting for transfers between devices, local(): gathered = lax.all_gather(hidden_low, 'mp', axis=0, tiled=True)  101 us
    all_gather x1, waiting for transfers between devices, local(): grad_gathered = lax.all_gather(grad_feed, 'mp', axis=0, tiled=True)  100 us
    reshape x2, local copies, waits for them, and re-layouts, toeplitz(): return tiled.reshape(head_count, length, span - 1)[:, :, :length]  89.2 us
    unnamed x130, local copies, waits for them, and re-layouts  59.4 us
    another operation x2, local copies, waits for them, and re-layouts, toeplitz(): tiled = jnp.tile(rolled, (1, length))[:, :length * (span - 1)]  49.6 us
  transfers between devices with their start and end apart: 7, of which 7 were waited for; matrix products, arithmetic and copies ran while one was open for 14% of the time, Pallas kernels for 0%

commit v1 on v0

--- a/solution.py
+++ b/solution.py
@@ -4,6 +4,22 @@
 from jax.sharding import PartitionSpec as P
 
 EPSILON = 1e-05
+
+
+def gather_around(x, axis, dim):
+    ways, here, step = (lax.axis_size(axis), lax.axis_index(axis), x.shape[dim])
+    dims = [n * ways if d == dim else n for d, n in enumerate(x.shape)]
+    full = lax.dynamic_update_slice_in_dim(jnp.zeros(dims, x.dtype), x, here * step, axis=dim)
+    going_up = going_down = x
+    for far in range(1, ways // 2 + 1):
+        going_up = lax.ppermute(going_up, axis, [(d, (d + 1) % ways) for d in range(ways)])
+        full = lax.dynamic_update_slice_in_dim(full, going_up, (here - far) % ways * step, axis=dim)
+        if 2 * far < ways:
+            going_down = lax.ppermute(going_down, axis, [(d, (d - 1) % ways) for d in range(ways)])
+            full = lax.dynamic_update_slice_in_dim(
+                full, going_down, (here + far) % ways * step, axis=dim
+            )
+    return full
 
 
 def dot_first(left_side, right_side):
@@ -154,7 +170,7 @@
         token_rows.astype(jnp.float32) + branch, first_factor, first_shift.astype(jnp.float32)
     )
     hidden_low = hidden.astype(jnp.bfloat16)
-    gathered = lax.all_gather(hidden_low, "mp", axis=0, tiled=True)
+    gathered = gather_around(hidden_low, "mp", 0)
     upward = jnp.dot(gathered, up_weight, preferred_element_type=jnp.float32) + up_bias.astype(
         jnp.float32
     )

time: 1380 us -> 1430 us (1.036)
  starting transfers between devices: 0.69 us -> 103 us
  waiting for transfers between devices: 860 us -> 784 us
  local copies, waits for them, and re-layouts: 320 us -> 345 us
    ppermute x0 -> x15, starting transfers between devices: none -> 102 us  [the longest x8 99.2 us: gather_around(): lax.ppermute(going_up, axis, [(d, (d + 1) % ways) for d in range(ways)])]
    all_gather x1 -> x0, waiting for transfers between devices: 101 us -> none  [local(): gathered = lax.all_gather(hidden_low, 'mp', axis=0, tiled=True)]
    ppermute x0 -> x15, waiting for transfers between devices: none -> 21.5 us  [the longest x8 21.5 us: gather_around(): lax.ppermute(going_up, axis, [(d, (d + 1) % ways) for d in range(ways)])]
    dynamic_update_slice x0 -> x15, local copies, waits for them, and re-layouts: none -> 21.2 us  [the longest x8 11.1 us: gather_around(): lax.dynamic_update_slice_in_dim(full, going_up, (here - far) % ways * ste...]
    unnamed x130 -> x154, local copies, waits for them, and re-layouts: 59.4 us -> 58.3 us
  transfers between devices with their start and end apart: 7 -> 21, of which waited for: 7 -> 11; matrix products, arithmetic and copies ran while one was open for 14% -> 15% of each run, Pallas kernels for 0% -> 0%
where the time goes in v1:
time: 1430 us
  waiting for transfers between devices  784 us (55%)
  local copies, waits for them, and re-layouts  345 us (24%)
  matrix products  140 us (10%)
  starting transfers between devices  103 us (7%)
  other arithmetic  34.8 us (2%)
  between operations  15.8 us (1%)
    reduce_scatter x1, waiting for transfers between devices, local(): lax.psum_scatter(jnp.dot(activated, down_weight, preferred_element_type=j...  246 us
    reduce_scatter x1, waiting for transfers between devices, local(): lax.psum_scatter(dot_last(grad_upward, up_weight), 'mp', scatter_dimensio...  241 us
    psum x2, waiting for transfers between devices, local(): lax.psum((grad_query_weight, grad_query_bias, grad_key_weight, grad_value...  139 us
    all_gather x1, waiting for transfers between devices, local(): grad_gathered = lax.all_gather(grad_feed, 'mp', axis=0, tiled=True)  100 us
    ppermute x8, starting transfers between devices, gather_around(): lax.ppermute(going_up, axis, [(d, (d + 1) % ways) for d in range(ways)])  99.2 us
    reshape x2, local copies, waits for them, and re-layouts, toeplitz(): return tiled.reshape(head_count, length, span - 1)[:, :, :length]  89.3 us
    unnamed x154, local copies, waits for them, and re-layouts  58.3 us
    another operation x2, local copies, waits for them, and re-layouts, toeplitz(): tiled = jnp.tile(rolled, (1, length))[:, :length * (span - 1)]  49.6 us
  transfers between devices with their start and end apart: 21, of which 11 were waited for; matrix products, arithmetic and copies ran while one was open for 15% of the time, Pallas kernels for 0%

profile of v1, /device:TPU:8, one launch (start us, length us, event | category | flops | bytes accessed | tf_op | source)
XLA Modules:
  0.0 1428.2 jit_solution(3226191657664535763)
XLA Ops:
  20.0 11.5 tile.4
  31.5 38.1 %tile.10 = f32[12,523776]{1,0:T(8,128)} reshape(f32[12,512,1023]{2,1,0:T(8,128)} %tile.4) | data formatting | bytes 50282496 | tf_op jit(solution)/shard_map/tile | solution.py:41
  69.6 22.6 %slice.28 = f32[12,523264]{1,0:T(8,128)} slice(f32[12,523776]{1,0:T(8,128)} %tile.10), slice={[0:12], [0:523264]} | slice | bytes 50233344 | tf_op jit(solution)/shard_map/slice | solution.py:41
  92.1 42.3 %reshape.182 = f32[12,512,1022]{2,1,0:T(8,128)} reshape(f32[12,523264]{1,0:T(8,128)} %slice.28) | data formatting | bytes 50233344 | tf_op jit(solution)/shard_map/reshape | solution.py:42
  134.4 10.6 slice.29
  145.0 12.6 copy.112
  211.6 13.3 collective-permute-start.4
  226.8 17.1 %collective-permute-start.6 = (bf16[512,768]{1,0:T(8,128)(2,1)S(1)}, bf16[512,768]{1,0:T(8,128)(2,1)S(1)}, u32[]{:S(2)}, u32[]{:S(2)}) collective-permute-start(bf16[512,768]{1,0:T(8,128)(2,1)S(1)} %collective-permute-done.4), channel_id=1, source_target_pairs={{0,1},{1,2},{2,3},{3,4},{4,5},{5,6},{6,7},{7,8},{8,9},{9,10},{10,1... | collective-permute-start | bytes 2359304 | tf_op jit(solution)/shard_map/ppermute | solution.py:15
  245.9 15.9 %collective-permute-start.8 = (bf16[512,768]{1,0:T(8,128)(2,1)S(1)}, bf16[512,768]{1,0:T(8,128)(2,1)}, u32[]{:S(2)}, u32[]{:S(2)}) collective-permute-start(bf16[512,768]{1,0:T(8,128)(2,1)S(1)} %collective-permute-done.6), channel_id=1, source_target_pairs={{0,1},{1,2},{2,3},{3,4},{4,5},{5,6},{6,7},{7,8},{8,9},{9,10},{10,1... | collective-permute-start | bytes 2359304 | tf_op jit(solution)/shard_map/ppermute | solution.py:15
  264.0 17.1 %collective-permute-start.10 = (bf16[512,768]{1,0:T(8,128)(2,1)}, bf16[512,768]{1,0:T(8,128)(2,1)}, u32[]{:S(2)}, u32[]{:S(2)}) collective-permute-start(bf16[512,768]{1,0:T(8,128)(2,1)} %collective-permute-done.8), channel_id=1, source_target_pairs={{0,1},{1,2},{2,3},{3,4},{4,5},{5,6},{6,7},{7,8},{8,9},{9,10},{10,1... | collective-permute-start | bytes 2359304 | tf_op jit(solution)/shard_map/ppermute | solution.py:15
  285.4 15.9 %collective-permute-start.12 = (bf16[512,768]{1,0:T(8,128)(2,1)}, bf16[512,768]{1,0:T(8,128)(2,1)S(1)}, u32[]{:S(2)}, u32[]{:S(2)}) collective-permute-start(bf16[512,768]{1,0:T(8,128)(2,1)} %collective-permute-done.10), channel_id=1, source_target_pairs={{0,1},{1,2},{2,3},{3,4},{4,5},{5,6},{6,7},{7,8},{8,9},{9,10},{10,1... | collective-permute-start | bytes 2359304 | tf_op jit(solution)/shard_map/ppermute | solution.py:15
  308.2 13.3 collective-permute-start.14
  331.5 20.5 %multiply_convert_fusion.1 = (bf16[8192,192]{0,1:T(8,128)(2,1)S(1)}, f32[8192,192]{0,1:T(8,128)}, f32[8192,192]{0,1:T(8,128)}) fusion(f32[192]{0:T(256)S(1)} %convert_element_type.196, bf16[8192,768]{1,0:T(8,128)(2,1)} %constant_dynamic-update-slice_fusion, bf16[768,192]{0,1:T(8,128)(2,1)S(1)} %copy-done.44), kind=kOutput, calls=%fused_computation.9 | convolution fusion | flops 2519728128 | bytes 28607232 | tf_op jit(solution)/shard_map/dot_general | solution.py:174
  364.7 245.5 %reduce-scatter.3.cloned.1.call-done = f32[512,768]{1,0:T(8,128)} async-done(((f32[8192,768]{1,0:T(8,128)}), f32[512,768]{1,0:T(8,128)}) %reduce-scatter.3.cloned.1.call-update) | async-done | bytes 1572880 | tf_op jit(solution)/shard_map/reduce_scatter | solution.py:178
  618.2 100.3 %all-gather.2.cloned.1.call-done = bf16[8192,768]{1,0:T(8,128)(2,1)} async-done(((bf16[512,768]{1,0:T(8,128)(2,1)}), bf16[8192,768]{1,0:T(8,128)(2,1)}) %all-gather.2.cloned.1.call-update) | async-done | bytes 12582928 | tf_op jit(solution)/shard_map/all_gather | solution.py:199
  744.3 240.8 %reduce-scatter.5.cloned.1.call-done = f32[512,768]{1,0:T(8,128)} async-done(((f32[8192,768]{1,0:T(8,128)}), f32[512,768]{1,0:T(8,128)}) %reduce-scatter.5.cloned.1.call-update) | async-done | bytes 1572880 | tf_op jit(solution)/shard_map/reduce_scatter | solution.py:205
  1001.5 18.3 %fusion = (f32[12,512,512]{1,2,0:T(8,128)}, bf16[12,512,512]{1,2,0:T(8,128)(2,1)}) fusion(f32[12,512,512]{1,2,0:T(8,128)} %get-tuple-element.154, f32[12,512]{1,0:T(8,128)S(1)} %negate_divide_fusion, f32[512,512]{0,1:T(8,128)} %compare_convert_fusion, f32[12,512,512]{1,2,0:T(8,128)} %copy.112, bf16[512,12,64]{0,2,1:T(8,128)(2,1)} %bitcast.162, ...), kind=kOutput, calls=%fused_computation.3 | convolution fusion | flops 419561472 | bytes 46710784 | tf_op jit(solution)/shard_map/while/body/eval_jaxpr/lhd,khd->hlk/dot_general | solution.py:238
  1060.0 12.7 copy.113
  1072.7 14.7 %pad.14.clone = f32[12,512,1022]{2,1,0:T(8,128)} pad(f32[12,512,512]{2,1,0:T(8,128)} %copy.113, f32[]{:T(128)} %constant.191.clone.1), padding=0_0x0_0x0_510 | pad | bytes 37699588 | tf_op jit(solution)/shard_map/transpose(jvp())/pad | solution.py:42
  1087.4 47.0 %reshape.189 = f32[12,523264]{1,0:T(8,128)} reshape(f32[12,512,1022]{2,1,0:T(8,128)} %pad.14.clone) | data formatting | bytes 50233344 | tf_op jit(solution)/shard_map/transpose(jvp())/reshape | solution.py:42
  1134.4 22.9 %pad.15 = f32[12,523776]{1,0:T(8,128)} pad(f32[12,523264]{1,0:T(8,128)} %reshape.189, f32[]{:T(128)} %constant.191.clone.1), padding=0_0x0_512 | pad | bytes 50257924 | tf_op jit(solution)/shard_map/transpose(jvp())/pad | solution.py:41
  1157.4 43.9 %reshape.190 = f32[12,512,1023]{2,1,0:T(8,128)} reshape(f32[12,523776]{1,0:T(8,128)} %pad.15) | data formatting | bytes 50282496 | tf_op jit(solution)/shard_map/transpose(jvp())/reshape | solution.py:41
  1236.1 36.7 %all-reduce.15.cloned.1.call-done = (f32[768,192]{0,1:T(8,128)}, f32[192,768]{1,0:T(8,128)}) async-done(((f32[768,192]{0,1:T(8,128)}, f32[192,768]{1,0:T(8,128)}), (f32[768,192]{0,1:T(8,128)}, f32[192,768]{1,0:T(8,128)})) %all-reduce.15.cloned.1.call-update) | async-done | bytes 1179664 | tf_op jit(solution)/shard_map/psum | solution.py:208
  1272.8 136.6 %all-reduce.11.cloned.1.call-done = (f32[768]{0:T(1024)}, f32[768]{0:T(1024)}, f32[768]{0:T(1024)}, f32[12,1023]{1,0:T(8,128)}, f32[768]{0:T(1024)}, /*index=5*/...) async-done(((f32[768]{0:T(1024)}, f32[768]{0:T(1024)}, f32[768]{0:T(1024)}, f32[12,1023]{1,0:T(8,128)}, f32[768]{0:T(1024)}, /*index=5*/f32[768]{0:T(1024)}, ...) | async-done | bytes 73696 | tf_op jit(solution)/shard_map/psum | solution.py:286
  (285 shorter events, 242.2 us)
Async XLA Ops:
  7.2 157.0 %copy-start = (bf16[8,12,64,64]{3,2,1,0:T(8,128)(2,1)S(1)}, bf16[8,12,64,64]{3,2,1,0:T(8,128)(2,1)}, u32[]{:S(2)}) copy-start(bf16[8,12,64,64]{3,2,1,0:T(8,128)(2,1)} %param.24) | copy-start | bytes 2359300
  7.2 603.0 %reduce-scatter.3.cloned.1.call-start = ((), (), s32[]{:S(2)}) async-start(), calls=%async_computation.2 | async-start | bytes 26738688 | tf_op jit(solution)/shard_map/reduce_scatter | solution.py:178
  14.2 150.0 %copy-start.10 = (bf16[512,768]{0,1:T(8,128)(2,1)}, bf16[512,768]{0,1:T(8,128)(2,1)S(1)}, u32[]{:S(2)}) copy-start(bf16[512,768]{0,1:T(8,128)(2,1)S(1)} %copy.58) | copy-start | bytes 2359300
  18.9 145.9 %copy-start.12 = (bf16[512,768]{0,1:T(8,128)(2,1)}, bf16[512,768]{0,1:T(8,128)(2,1)S(1)}, u32[]{:S(2)}) copy-start(bf16[512,768]{0,1:T(8,128)(2,1)S(1)} %copy.60) | copy-start | bytes 2359300
  185.9 12.4 collective-permute-start
  185.9 19.0 %collective-permute-start.1 = (bf16[512,768]{1,0:T(8,128)(2,1)S(1)}, bf16[512,768]{1,0:T(8,128)(2,1)S(1)}, u32[]{:S(2)}, u32[]{:S(2)}) collective-permute-start(bf16[512,768]{1,0:T(8,128)(2,1)S(1)} %get-tuple-element.148), channel_id=1, source_target_pairs={{0,15},{1,0},{2,1},{3,2},{4,3},{5,4},{6,5},{7,6},{8,7},{9,8},{10,9... | collective-permute-start | bytes 2359304 | tf_op jit(solution)/shard_map/ppermute | solution.py:18
  198.3 12.4 collective-permute-start.2
  205.0 19.9 %collective-permute-start.3 = (bf16[512,768]{1,0:T(8,128)(2,1)S(1)}, bf16[512,768]{1,0:T(8,128)(2,1)S(1)}, u32[]{:S(2)}, u32[]{:S(2)}) collective-permute-start(bf16[512,768]{1,0:T(8,128)(2,1)S(1)} %collective-permute-done.1), channel_id=1, source_target_pairs={{0,15},{1,0},{2,1},{3,2},{4,3},{5,4},{6,5},{7,6},{8,7},{9,8},{10,9... | collective-permute-start | bytes 2359304 | tf_op jit(solution)/shard_map/ppermute | solution.py:18
  211.6 15.2 %collective-permute-start.4 = (bf16[512,768]{1,0:T(8,128)(2,1)S(1)}, bf16[512,768]{1,0:T(8,128)(2,1)S(1)}, u32[]{:S(2)}, u32[]{:S(2)}) collective-permute-start(bf16[512,768]{1,0:T(8,128)(2,1)S(1)} %collective-permute-done.2), channel_id=1, source_target_pairs={{0,1},{1,2},{2,3},{3,4},{4,5},{5,6},{6,7},{7,8},{8,9},{9,10},{10,1... | collective-permute-start | bytes 2359304 | tf_op jit(solution)/shard_map/ppermute | solution.py:15
  224.9 19.1 %collective-permute-start.5 = (bf16[512,768]{1,0:T(8,128)(2,1)S(1)}, bf16[512,768]{1,0:T(8,128)(2,1)S(1)}, u32[]{:S(2)}, u32[]{:S(2)}) collective-permute-start(bf16[512,768]{1,0:T(8,128)(2,1)S(1)} %collective-permute-done.3), channel_id=1, source_target_pairs={{0,15},{1,0},{2,1},{3,2},{4,3},{5,4},{6,5},{7,6},{8,7},{9,8},{10,9... | collective-permute-start | bytes 2359304 | tf_op jit(solution)/shard_map/ppermute | solution.py:18
  226.8 19.1 %collective-permute-start.6 = (bf16[512,768]{1,0:T(8,128)(2,1)S(1)}, bf16[512,768]{1,0:T(8,128)(2,1)S(1)}, u32[]{:S(2)}, u32[]{:S(2)}) collective-permute-start(bf16[512,768]{1,0:T(8,128)(2,1)S(1)} %collective-permute-done.4), channel_id=1, source_target_pairs={{0,1},{1,2},{2,3},{3,4},{4,5},{5,6},{6,7},{7,8},{8,9},{9,10},{10,1... | collective-permute-start | bytes 2359304 | tf_op jit(solution)/shard_map/ppermute | solution.py:15
  244.0 17.8 %collective-permute-start.7 = (bf16[512,768]{1,0:T(8,128)(2,1)S(1)}, bf16[512,768]{1,0:T(8,128)(2,1)}, u32[]{:S(2)}, u32[]{:S(2)}) collective-permute-start(bf16[512,768]{1,0:T(8,128)(2,1)S(1)} %collective-permute-done.5), channel_id=1, source_target_pairs={{0,15},{1,0},{2,1},{3,2},{4,3},{5,4},{6,5},{7,6},{8,7},{9,8},{10,9... | collective-permute-start | bytes 2359304 | tf_op jit(solution)/shard_map/ppermute | solution.py:18
  245.9 18.1 %collective-permute-start.8 = (bf16[512,768]{1,0:T(8,128)(2,1)S(1)}, bf16[512,768]{1,0:T(8,128)(2,1)}, u32[]{:S(2)}, u32[]{:S(2)}) collective-permute-start(bf16[512,768]{1,0:T(8,128)(2,1)S(1)} %collective-permute-done.6), channel_id=1, source_target_pairs={{0,1},{1,2},{2,3},{3,4},{4,5},{5,6},{6,7},{7,8},{8,9},{9,10},{10,1... | collective-permute-start | bytes 2359304 | tf_op jit(solution)/shard_map/ppermute | solution.py:15
  261.8 21.5 %collective-permute-start.9 = (bf16[512,768]{1,0:T(8,128)(2,1)}, bf16[512,768]{1,0:T(8,128)(2,1)}, u32[]{:S(2)}, u32[]{:S(2)}) collective-permute-start(bf16[512,768]{1,0:T(8,128)(2,1)} %collective-permute-done.7), channel_id=1, source_target_pairs={{0,15},{1,0},{2,1},{3,2},{4,3},{5,4},{6,5},{7,6},{8,7},{9,8},{10,9... | collective-permute-start | bytes 2359304 | tf_op jit(solution)/shard_map/ppermute | solution.py:18
  264.0 21.5 %collective-permute-start.10 = (bf16[512,768]{1,0:T(8,128)(2,1)}, bf16[512,768]{1,0:T(8,128)(2,1)}, u32[]{:S(2)}, u32[]{:S(2)}) collective-permute-start(bf16[512,768]{1,0:T(8,128)(2,1)} %collective-permute-done.8), channel_id=1, source_target_pairs={{0,1},{1,2},{2,3},{3,4},{4,5},{5,6},{6,7},{7,8},{8,9},{9,10},{10,1... | collective-permute-start | bytes 2359304 | tf_op jit(solution)/shard_map/ppermute | solution.py:15
  283.3 22.8 %collective-permute-start.11 = (bf16[512,768]{1,0:T(8,128)(2,1)}, bf16[512,768]{1,0:T(8,128)(2,1)S(1)}, u32[]{:S(2)}, u32[]{:S(2)}) collective-permute-start(bf16[512,768]{1,0:T(8,128)(2,1)} %collective-permute-done.9), channel_id=1, source_target_pairs={{0,15},{1,0},{2,1},{3,2},{4,3},{5,4},{6,5},{7,6},{8,7},{9,8},{10,9... | collective-permute-start | bytes 2359304 | tf_op jit(solution)/shard_map/ppermute | solution.py:18
  285.4 22.7 %collective-permute-start.12 = (bf16[512,768]{1,0:T(8,128)(2,1)}, bf16[512,768]{1,0:T(8,128)(2,1)S(1)}, u32[]{:S(2)}, u32[]{:S(2)}) collective-permute-start(bf16[512,768]{1,0:T(8,128)(2,1)} %collective-permute-done.10), channel_id=1, source_target_pairs={{0,1},{1,2},{2,3},{3,4},{4,5},{5,6},{6,7},{7,8},{8,9},{9,10},{10,1... | collective-permute-start | bytes 2359304 | tf_op jit(solution)/shard_map/ppermute | solution.py:15
  306.1 23.5 %collective-permute-start.13 = (bf16[512,768]{1,0:T(8,128)(2,1)S(1)}, bf16[512,768]{1,0:T(8,128)(2,1)S(1)}, u32[]{:S(2)}, u32[]{:S(2)}) collective-permute-start(bf16[512,768]{1,0:T(8,128)(2,1)S(1)} %collective-permute-done.11), channel_id=1, source_target_pairs={{0,15},{1,0},{2,1},{3,2},{4,3},{5,4},{6,5},{7,6},{8,7},{9,8},{10,9... | collective-permute-start | bytes 2359304 | tf_op jit(solution)/shard_map/ppermute | solution.py:18
  308.2 22.4 %collective-permute-start.14 = (bf16[512,768]{1,0:T(8,128)(2,1)S(1)}, bf16[512,768]{1,0:T(8,128)(2,1)S(1)}, u32[]{:S(2)}, u32[]{:S(2)}) collective-permute-start(bf16[512,768]{1,0:T(8,128)(2,1)S(1)} %collective-permute-done.12), channel_id=1, source_target_pairs={{0,1},{1,2},{2,3},{3,4},{4,5},{5,6},{6,7},{7,8},{8,9},{9,10},{10,1... | collective-permute-start | bytes 2359304 | tf_op jit(solution)/shard_map/ppermute | solution.py:15
  364.0 354.5 %all-gather.2.cloned.1.call-start = ((), (), s32[]{:S(2)}) async-start(), calls=%async_computation.3 | async-start | bytes 13369344 | tf_op jit(solution)/shard_map/all_gather | solution.py:199
  618.1 367.0 %reduce-scatter.5.cloned.1.call-start = ((), (), s32[]{:S(2)}) async-start(), calls=%async_computation.4 | async-start | bytes 26738688 | tf_op jit(solution)/shard_map/reduce_scatter | solution.py:205
  743.9 483.0 %all-reduce.13.cloned.1.call-start = ((), (), s32[]{:S(2)}) async-start(), calls=%async_computation.6 | async-start | bytes 18874368 | tf_op jit(solution)/shard_map/psum | solution.py:286
  1034.9 237.9 %all-reduce.15.cloned.1.call-start = ((), (), s32[]{:S(2)}) async-start(), calls=%async_computation.7 | async-start | bytes 2359296 | tf_op jit(solution)/shard_map/psum | solution.py:208
  1059.9 349.4 %all-reduce.11.cloned.1.call-start = ((), (), s32[]{:S(2)}) async-start(), calls=%async_computation.5 | async-start | bytes 196608 | tf_op jit(solution)/shard_map/psum | solution.py:286
  (66 other events, 535.5 us)
Sparse Core Ops, SparseCore 0:
  364.1 246.0 reduce-scatter.2
  618.3 100.2 all-gather.1
  744.0 241.0 reduce-scatter.4
  1035.0 191.8 all-reduce.12
  1229.7 42.9 all-reduce.14
  1280.7 128.6 all-reduce.10
